TPU v7x, 32 devices: a whole 2x2x4 slice. The times are simulated.
32 devices in a mesh: groups: 2 (over y), expert: 4 (over x, core), replica: 4 (over z).
Axes of the slice: x: 2, y: 2, z: 4, core: 2. Of those that a mesh axis runs over, the one named last changes fastest.
Arguments:
- tokens: bfloat16 [768, 7168], P(('groups', 'expert'), 'replica'), parts along dimension 0, may hold values from -6 to 6
- expert_ids: int32 [768, 2], P(('groups', 'expert')), parts along dimension 0, may hold values from 0 to 3, all different within a row; in each aligned block of 96 rows (0 to 95, 96 to 191, ...) at most 60 rows name the same one
- affinity: float32 [768, 2], P(('groups', 'expert')), parts along dimension 0, may hold values from 0.05 to 1
- gate_up: bfloat16 [4, 7168, 2, 2048], P('expert', 'replica'), may hold values from -0.0625 to 0.0625
- down_proj: bfloat16 [4, 2048, 7168], P('expert', None, 'replica'), may hold values from -0.125 to 0.125
Outputs:
- mixed: bfloat16 [768, 7168], P(('groups', 'expert'), 'replica'), parts along dimension 0
There are 2 independent parts, one for each index of `groups`. A program takes and returns all parts, laid end to end along the dimension named above; an argument that names none is the same for every part. Nothing has to cross between parts.
Inputs may be any that keep to these rules, and one draw needn't show every extreme that they name: `expert_ids`: each row names 2 different experts. Within each aligned block of 96 rows no expert is named by more than 60 rows, a bound that some block reaches.
All inputs are finite; a program needn't handle non-finite values.
Results may differ from a plain program's by a relative error of at most 0.023.
Values may be sent and summed in bfloat16 or wider, within the bound.
No kernel may reach another device: no remote copies, remote signals or barrier semaphores. Data moves between devices by JAX's collectives and lax.ppermute only.
A program may use at most 128 MiB of HBM per device.

v0:
```python
import jax
import jax.numpy as jnp
from jax import lax
from jax.sharding import PartitionSpec as P


def slot_table(expert_ids, expert_count, capacity):
    labels = lax.broadcasted_iota(jnp.int32, (1, 1, expert_count), 2)
    chosen = (expert_ids[:, :, None] == labels).astype(jnp.int32)
    per_row = jnp.sum(chosen, axis=1)
    before = jnp.cumsum(per_row, axis=0) - per_row
    slot_rank = jnp.sum(chosen * before[:, None, :], axis=2)
    return expert_ids * capacity + slot_rank


def per_device(tokens, expert_ids, affinity, gate_up, down_proj):
    expert_count = lax.axis_size("expert")
    row_count, top_count = expert_ids.shape
    capacity = 5 * row_count * top_count // (4 * expert_count)
    width_local = tokens.shape[1]
    hidden_width = down_proj.shape[1]
    slot_index = slot_table(expert_ids, expert_count, capacity)
    row_labels = jnp.broadcast_to(
        lax.broadcasted_iota(jnp.int32, (row_count, 1), 0), (row_count, top_count)
    )
    source = (
        jnp.full((expert_count * capacity,), row_count, jnp.int32)
        .at[slot_index.reshape(-1)]
        .set(row_labels.reshape(-1))
    )
    padded = jnp.concatenate([tokens, jnp.zeros((1, width_local), tokens.dtype)], axis=0)
    outgoing = padded[source].reshape(expert_count, capacity, width_local)
    pair_weight = gate_up[0].reshape(width_local, 2 * hidden_width)
    down_local = down_proj[0]
    slot_block = lax.all_to_all(outgoing, "expert", split_axis=0, concat_axis=0, tiled=True)
    group_count, item_count, feature_count = slot_block.shape
    partial_sum = jnp.dot(
        slot_block.reshape(group_count * item_count, feature_count),
        pair_weight,
        preferred_element_type=jnp.float32,
    )
    partial_rows = partial_sum.astype(jnp.bfloat16).reshape(
        group_count, item_count, 2, hidden_width
    )
    summed = lax.psum(partial_rows, "replica").astype(jnp.float32)
    hidden = (jax.nn.silu(summed[:, :, 0]) * summed[:, :, 1]).astype(jnp.bfloat16)
    result = jnp.dot(
        hidden.reshape(-1, hidden_width), down_local, preferred_element_type=jnp.float32
    )
    expert_rows = result.astype(jnp.bfloat16).reshape(expert_count, capacity, width_local)
    returned = lax.all_to_all(expert_rows, "expert", split_axis=0, concat_axis=0, tiled=True)
    picked = returned.reshape(expert_count * capacity, width_local)[slot_index]
    weights = 2.5 * affinity / jnp.sum(affinity, axis=1, keepdims=True)
    mixed = jnp.einsum("tk,tkd->td", weights, picked.astype(jnp.float32))
    return mixed.astype(jnp.bfloat16)


def solution(mesh):
    placed = (
        P(("groups", "expert"), "replica"),
        P(("groups", "expert"), None),
        P(("groups", "expert"), None),
        P("expert", "replica", None, None),
        P("expert", None, "replica"),
    )
    return jax.shard_map(
        per_device,
        mesh=mesh,
        in_specs=placed,
        out_specs=P(("groups", "expert"), "replica"),
        check_vma=False,
    )
```

profile of v0, /device:TPU:0, one launch (start us, length us, event | category | flops | bytes accessed | tf_op | source)
XLA Modules:
  0.0 176.3 jit_solution(14017311911551673025)
XLA Ops:
  6.5 0.7 convert_reduce_fusion
  7.5 0.7 select_reduce_fusion
  8.3 0.7 compare_select_fusion.1
  9.3 1.2 scatter_custom_fusion
  10.6 1.0 concatenate.3
  11.6 1.3 gather_fusion
  12.9 1.1 reshape.66
  14.0 4.2 %all-to-all-start = ((bf16[4,60,1792]{2,1,0:T(8,128)(2,1)}), bf16[4,60,1792]{2,1,0:T(8,128)(2,1)S(1)}, u32[]{:S(2)}, u32[]{:S(2)}) async-start(bf16[4,60,1792]{2,1,0:T(8,128)(2,1)} %reshape.66), calls=%async_computation | async-start | bytes 1835008 | tf_op jit(solution)/shard_map/all_to_all | solution.py:35
  18.2 16.1 %copy.19 = bf16[224,8,2,2048]{3,1,2,0:T(8,128)(2,1)} copy(bf16[224,8,2,2048]{3,2,1,0:T(2,128)(2,1)} %bitcast.21) | data formatting | bytes 29360128
  34.5 10.3 %convolution_convert_fusion = bf16[240,4096]{1,0:T(8,128)(2,1)} fusion(bf16[240,1792]{1,0:T(8,128)(2,1)S(1)} %reshape.67, bf16[1792,4096]{1,0:T(8,128)(2,1)} %bitcast.22), kind=kOutput, calls=%fused_computation.5 | convolution fusion | flops 3524198400 | bytes 17506304 | tf_op jit(solution)/shard_map/dot_general | solution.py:37
  44.9 4.8 %reshape.68 = bf16[4,60,2,2048]{3,2,1,0:T(2,128)(2,1)S(1)} reshape(bf16[240,4096]{1,0:T(8,128)(2,1)} %convolution_convert_fusion) | data formatting | bytes 3932160 | tf_op jit(solution)/shard_map/reshape | solution.py:42
  49.7 2.1 %copy.15 = bf16[4,60,2,2048]{3,1,0,2:T(8,128)(2,1)} copy(bf16[4,60,2,2048]{3,2,1,0:T(2,128)(2,1)S(1)} %reshape.68) | data formatting | bytes 3932160 | tf_op jit(solution)/shard_map/reshape | solution.py:42
  51.9 88.8 %all-reduce.3.cloned.1.call-done = bf16[4,60,2,2048]{3,1,0,2:T(8,128)(2,1)} async-done(((bf16[4,60,2,2048]{3,1,0,2:T(8,128)(2,1)}), bf16[4,60,2,2048]{3,1,0,2:T(8,128)(2,1)}) %all-reduce.3.cloned.1.call-update) | async-done | bytes 1966096 | tf_op jit(solution)/shard_map/psum | solution.py:45
  140.6 2.1 %convert_element_type.25 = f32[4,60,2,2048]{3,1,0,2:T(8,128)S(1)} convert(bf16[4,60,2,2048]{3,1,0,2:T(8,128)(2,1)} %all-reduce.3.cloned.1.call-done) | non-fusion elementwise | flops 983040 | bytes 5898240 | tf_op jit(solution)/shard_map/convert_element_type | solution.py:45
  142.7 0.6 fusion.5
  143.4 0.2 convert_element_type.27
  143.6 5.0 %fusion.2 = bf16[240,1792]{1,0:T(8,128)(2,1)S(1)} fusion(bf16[240,2048]{1,0:T(8,128)(2,1)S(1)} %convert_element_type.27, bf16[1,2048,1792]{2,1,0:T(8,128)(2,1)} %param.9), kind=kOutput, calls=%fused_computation.6 | convolution fusion | flops 1762037760 | bytes 9183232 | tf_op jit(solution)/shard_map/dot_general | solution.py:47
  148.6 1.1 reshape.69
  149.7 3.5 %all-to-all-start.1 = ((bf16[4,60,1792]{2,1,0:T(8,128)(2,1)}), bf16[4,60,1792]{2,1,0:T(8,128)(2,1)S(1)}, u32[]{:S(2)}, u32[]{:S(2)}) async-start(bf16[4,60,1792]{2,1,0:T(8,128)(2,1)} %reshape.69), calls=%async_computation.1 | async-start | bytes 1835008 | tf_op jit(solution)/shard_map/all_to_all | solution.py:51
  153.7 12.6 %all-to-all-done.1 = bf16[4,60,1792]{2,1,0:T(8,128)(2,1)S(1)} async-done(((bf16[4,60,1792]{2,1,0:T(8,128)(2,1)}), bf16[4,60,1792]{2,1,0:T(8,128)(2,1)S(1)}, u32[]{:S(2)}, u32[]{:S(2)}) %all-to-all-start.1) | async-done | bytes 860192 | tf_op jit(solution)/shard_map/all_to_all | solution.py:51
  166.4 1.1 gather_fusion.1
  167.6 0.3 reshape.80
  167.8 0.9 fusion.8
  168.7 0.8 copy.21
  (24 shorter events, 1.5 us)
Async XLA Ops:
  14.0 20.4 %all-to-all-start = ((bf16[4,60,1792]{2,1,0:T(8,128)(2,1)}), bf16[4,60,1792]{2,1,0:T(8,128)(2,1)S(1)}, u32[]{:S(2)}, u32[]{:S(2)}) async-start(bf16[4,60,1792]{2,1,0:T(8,128)(2,1)} %reshape.66), calls=%async_computation | async-start | bytes 1835008 | tf_op jit(solution)/shard_map/all_to_all | solution.py:35
  18.2 122.4 %all-reduce.3.cloned.1.call-start = ((), (), s32[]{:S(2)}) async-start(), calls=%async_computation.2 | async-start | bytes 4194304 | tf_op jit(solution)/shard_map/psum | solution.py:45
  148.6 4.9 %copy-start = (f32[96,2]{0,1:T(2,128)S(1)}, f32[96,2]{0,1:T(2,128)}, u32[]{:S(2)}) copy-start(f32[96,2]{0,1:T(2,128)} %param.7) | copy-start | bytes 2308
  149.7 16.5 %all-to-all-start.1 = ((bf16[4,60,1792]{2,1,0:T(8,128)(2,1)}), bf16[4,60,1792]{2,1,0:T(8,128)(2,1)S(1)}, u32[]{:S(2)}, u32[]{:S(2)}) async-start(bf16[4,60,1792]{2,1,0:T(8,128)(2,1)} %reshape.69), calls=%async_computation.1 | async-start | bytes 1835008 | tf_op jit(solution)/shard_map/all_to_all | solution.py:51
Sparse Core Ops, SparseCore 0:
  52.0 88.6 all-reduce.2
where the time goes:
time: 177 us; the launch traced here: 176 us
  waiting for transfers between devices  101 us (57%)
  local copies, waits for them, and re-layouts  32.4 us (18%)
  matrix products  16.2 us (9%)
  between operations  13.6 us (8%)
  starting transfers between devices  7.74 us (4%)
  other arithmetic  5.03 us (3%)
    psum x1, waiting for transfers between devices, per_device(): summed = lax.psum(partial_rows, 'replica').astype(jnp.float32)  88.8 us
    unnamed x3, local copies, waits for them, and re-layouts  16.1 us
    all_to_all x1, waiting for transfers between devices, per_device(): lax.all_to_all(expert_rows, 'expert', split_axis=0, concat_axis=0, tiled=...  12.6 us
    dot_general x1, matrix products, per_device(): jnp.dot(slot_block.reshape(group_count * item_count, feature_count), pair...  10.3 us
    reshape x2, local copies, waits for them, and re-layouts, per_device(): partial_sum.astype(jnp.bfloat16)  6.97 us
    dot_general x1, matrix products, per_device(): jnp.dot(hidden.reshape(-1, hidden_width), down_local, preferred_element_t...  5.03 us
    all_to_all x1, starting transfers between devices, per_device(): lax.all_to_all(outgoing, 'expert', split_axis=0, concat_axis=0, tiled=True)  4.23 us
  transfers between devices with their start and end apart: 3, of which 2 were waited for; matrix products, arithmetic and copies ran while one was open for 9% of the time, Pallas kernels for 0%

commit v1 on v0

v1 whole, which is shorter than its diff:
```python
import jax
import jax.numpy as jnp
from jax import lax
from jax.experimental import pallas as pl
from jax.experimental.pallas import tpu as pltpu
from jax.sharding import PartitionSpec as P

F32, BF16, I32 = jnp.float32, jnp.bfloat16, jnp.int32


def routing(me, ids, experts):
    choices, rows = ids.shape
    label = me ^ lax.broadcasted_iota(I32, (experts, rows), 0)
    chosen = jnp.zeros((experts, rows), F32)
    for k in range(choices):
        chosen = chosen + (ids[k : k + 1] == label).astype(F32)
    earlier = lax.broadcasted_iota(I32, (rows, rows), 0) < lax.broadcasted_iota(I32, (rows, rows), 1)
    rank = jnp.dot(chosen.astype(BF16), earlier.astype(F32).astype(BF16), preferred_element_type=F32)
    slot = jnp.where(chosen > 0, rank.astype(I32), -1)
    return label, slot


def one_hot(slot_row, capacity):
    rows = slot_row.shape[1]
    return slot_row == lax.broadcasted_iota(I32, (capacity, rows), 0)


def dispatch_body(me_ref, ids_ref, tokens_ref, *out_refs):
    experts, capacity = len(out_refs), out_refs[0].shape[0]
    _, slot = routing(me_ref[0], ids_ref[...], experts)
    tokens = tokens_ref[...]
    for s, out in enumerate(out_refs):
        pick = one_hot(slot[s : s + 1], capacity).astype(F32).astype(BF16)
        out[...] = jnp.dot(pick, tokens, preferred_element_type=F32).astype(BF16)


def combine_body(me_ref, ids_ref, affinity_ref, *refs):
    *in_refs, out = refs
    experts, capacity = len(in_refs), in_refs[0].shape[0]
    ids, affinity = ids_ref[...], affinity_ref[...]
    label, slot = routing(me_ref[0], ids, experts)
    weights = 2.5 * affinity / jnp.sum(affinity, axis=0, keepdims=True)
    per_expert = jnp.zeros(label.shape, F32)
    for k in range(ids.shape[0]):
        per_expert = per_expert + jnp.where(ids[k : k + 1] == label, weights[k : k + 1], 0.0)
    total = jnp.zeros(out.shape, F32)
    for s, ref in enumerate(in_refs):
        rest = jnp.where(one_hot(slot[s : s + 1], capacity), per_expert[s : s + 1], 0.0)
        for _ in range(3):
            part = rest.astype(BF16)
            rest = rest - part.astype(F32)
            total = total + lax.dot_general(
                part, ref[...], (((0,), (0,)), ((), ())), preferred_element_type=F32
            )
    out[...] = total.astype(BF16)


def vmem(count):
    return [pl.BlockSpec(memory_space=pltpu.VMEM)] * count


def edge_pairs(count, parity, right, left):
    pairs = [(p, p + 1) for p in range(count - 1) if p % 2 == parity and right(p)]
    return pairs + [(p + 1, p) for p in range(count - 1) if p % 2 == parity and left(p + 1)]


def per_device(tokens, expert_ids, affinity, gate_up, down_proj):
    experts, replicas = lax.axis_size("expert"), lax.axis_size("replica")
    rows, choices = expert_ids.shape
    capacity = 5 * rows * choices // (4 * experts)
    width = tokens.shape[1]
    hidden_width = down_proj.shape[1]
    block = hidden_width // replicas
    me = lax.axis_index("expert").astype(I32)[None]
    here = lax.axis_index("replica")
    even = here % 2 == 0
    ids = expert_ids.T
    scalar = [pl.BlockSpec(memory_space=pltpu.SMEM)]

    slots = pl.pallas_call(
        dispatch_body,
        out_shape=[jax.ShapeDtypeStruct((capacity, width), BF16)] * experts,
        in_specs=scalar + vmem(2),
        out_specs=vmem(experts),
        name="dispatch",
    )(me, ids, tokens)

    def swap(x, s):
        return lax.ppermute(x, "expert", [(i, i ^ s) for i in range(experts)])

    arrived = [slots[0]] + [swap(slots[s], s) for s in range(1, experts)]
    x = jnp.concatenate(arrived, axis=0)
    weights = gate_up[0].reshape(width, 2 * hidden_width)
    partial = jnp.dot(x, weights, preferred_element_type=F32).astype(BF16)

    def columns(q):
        q = jnp.clip(q, 0, replicas - 1) * block
        g = lax.dynamic_slice(partial, (0, q), (x.shape[0], block))
        u = lax.dynamic_slice(partial, (0, hidden_width + q), (x.shape[0], block))
        return jnp.concatenate([g, u], axis=1).astype(F32)

    def hop(x, parity, right, left):
        pairs = edge_pairs(replicas, parity, right, left)
        return lax.ppermute(x, "replica", pairs) if pairs else jnp.zeros_like(x)

    got_a = got_b = None
    for s in range(1, replicas):
        to_right, to_left = replicas - s + here, here - replicas + s
        send_a = columns(jnp.where(even, to_right, to_left))
        send_b = columns(jnp.where(even, to_left, to_right))
        if s > 1:
            send_a, send_b = send_a + got_b.astype(F32), send_b + got_a.astype(F32)
        right, left = (lambda p: p <= s - 1), (lambda p: p >= replicas - s)
        got_a = hop(send_a.astype(BF16), 0, right, left)
        got_b = hop(send_b.astype(BF16), 1, right, left)
    pre = columns(here) + got_a.astype(F32) + got_b.astype(F32)
    hidden = (jax.nn.silu(pre[:, :block]) * pre[:, block:]).astype(BF16)

    def down(h, q):
        q = jnp.clip(q, 0, replicas - 1) * block
        part = lax.dynamic_slice(down_proj[0], (q, 0), (block, width))
        return jnp.dot(h, part, preferred_element_type=F32)

    result = down(hidden, here)
    send_a = send_b = hidden
    for s in range(1, replicas):
        right, left = (lambda p: p >= s - 1), (lambda p: p <= replicas - s)
        got_a = hop(send_a, 0, right, left)
        got_b = hop(send_b, 1, right, left)
        result = result + down(got_a, jnp.where(even, here + s, here - s))
        result = result + down(got_b, jnp.where(even, here - s, here + s))
        send_a, send_b = got_b, got_a
    back = result.astype(BF16).reshape(experts, capacity, width)
    returned = [back[0]] + [swap(back[s], s) for s in range(1, experts)]

    return pl.pallas_call(
        combine_body,
        out_shape=jax.ShapeDtypeStruct((rows, width), BF16),
        in_specs=scalar + vmem(2 + experts),
        out_specs=vmem(1)[0],
        name="combine",
    )(me, ids, affinity.T, *returned)


def solution(mesh):
    placed = (
        P(("groups", "expert"), "replica"),
        P(("groups", "expert"), None),
        P(("groups", "expert"), None),
        P("expert", "replica", None, None),
        P("expert", None, "replica"),
    )
    return jax.shard_map(
        per_device,
        mesh=mesh,
        in_specs=placed,
        out_specs=P(("groups", "expert"), "replica"),
        check_vma=False,
    )
```

time: 177 us -> 117 us (0.66)
  waiting for transfers between devices: 101 us -> 49.3 us
  starting transfers between devices: 7.74 us -> 22.7 us
  local copies, waits for them, and re-layouts: 32.4 us -> 18.7 us
  between operations: 13.6 us -> 0.23 us
  Pallas kernels: 0 us -> 5.72 us
    psum x1 -> x0, waiting for transfers between devices: 88.8 us -> none  [per_device(): summed = lax.psum(partial_rows, 'replica').astype(jnp.float32)]
    ppermute x0 -> x16, waiting for transfers between devices: none -> 49.3 us  [the longest x10 38.7 us: hop(): return lax.ppermute(x, 'replica', pairs) if pairs else jnp.zeros_like(x)]
    ppermute x0 -> x16, starting transfers between devices: none -> 22.7 us  [the longest x10 17.8 us: hop(): return lax.ppermute(x, 'replica', pairs) if pairs else jnp.zeros_like(x)]
    all_to_all x2 -> x0, waiting for transfers between devices: 12.6 us -> none  [the longest x1 12.6 us: per_device(): lax.all_to_all(expert_rows, 'expert', split_axis=0, concat_axis=0, tiled=...]
    reshape x8 -> x0, local copies, waits for them, and re-layouts: 9.74 us -> none  [the longest x2 6.97 us: per_device(): partial_sum.astype(jnp.bfloat16)]
    all_to_all x2 -> x0, starting transfers between devices: 7.74 us -> none  [the longest x1 4.23 us: per_device(): lax.all_to_all(outgoing, 'expert', split_axis=0, concat_axis=0, tiled=True)]
    pallas_call x0 -> x2, Pallas kernels: none -> 5.72 us  [the longest x1 3.45 us: per_device(): pl.pallas_call(combine_body, out_shape=jax.ShapeDtypeStruct((rows, width)...]
    gather x3 -> x0, local copies, waits for them, and re-layouts: 2.7 us -> none  [the longest x2 1.4 us: per_device(): picked = returned.reshape(expert_count * capacity, width_local)[slot_index]]
  transfers between devices with their start and end apart: 3 -> 16, of which waited for: 2 -> 8; matrix products, arithmetic and copies ran while one was open for 9% -> 21% of each run, Pallas kernels for 0% -> 0%
where the time goes in v1:
time: 117 us
  waiting for transfers between devices  49.3 us (42%)
  starting transfers between devices  22.7 us (19%)
  local copies, waits for them, and re-layouts  18.7 us (16%)
  matrix products  16.3 us (14%)
  Pallas kernels  5.72 us (5%)
  other arithmetic  3.88 us (3%)
    ppermute x10, waiting for transfers between devices, hop(): return lax.ppermute(x, 'replica', pairs) if pairs else jnp.zeros_like(x)  38.7 us
    ppermute x10, starting transfers between devices, hop(): return lax.ppermute(x, 'replica', pairs) if pairs else jnp.zeros_like(x)  17.8 us
    unnamed x15, local copies, waits for them, and re-layouts  16.8 us
    ppermute x6, waiting for transfers between devices, swap(): return lax.ppermute(x, 'expert', [(i, i ^ s) for i in range(experts)])  10.6 us
    dot_general x1, matrix products, per_device(): partial = jnp.dot(x, weights, preferred_element_type=F32).astype(BF16)  8.89 us
    dot_general x7, matrix products, down(): return jnp.dot(h, part, preferred_element_type=F32)  7.45 us
    ppermute x6, starting transfers between devices, swap(): return lax.ppermute(x, 'expert', [(i, i ^ s) for i in range(experts)])  4.94 us
    pallas_call x1, Pallas kernels, per_device(): pl.pallas_call(combine_body, out_shape=jax.ShapeDtypeStruct((rows, width)...  3.45 us
  transfers between devices with their start and end apart: 16, of which 8 were waited for; matrix products, arithmetic and copies ran while one was open for 21% of the time, Pallas kernels for 0%

profile of v1, /device:TPU:0, one launch (start us, length us, event | category | flops | bytes accessed | tf_op | source)
XLA Modules:
  0.0 116.9 jit_solution(11672286460860159157)
XLA Ops:
  0.0 2.3 %dispatch.1 = (bf16[60,1792]{1,0:T(8,128)(2,1)}, bf16[60,1792]{1,0:T(8,128)(2,1)}, bf16[60,1792]{1,0:T(8,128)(2,1)}, bf16[60,1792]{1,0:T(8,128)(2,1)}) custom-call(s32[1]{0:T(128)} %bitcast.me_ref, s32[2,96]{1,0:T(2,128)} %bitcast.38, bf16[96,1792]{1,0:T(8,128)(2,1)} %tokens_ref.1), custom_call_target="tpu_custom_call" | custom-call | tf_op jit(solution)/shard_map/dispatch/pallas_call | solution.py:80
  2.8 2.5 %collective-permute-start.1 = (bf16[60,1792]{1,0:T(8,128)(2,1)}, bf16[60,1792]{1,0:T(8,128)(2,1)S(1)}, u32[]{:S(2)}, u32[]{:S(2)}) collective-permute-start(bf16[60,1792]{1,0:T(8,128)(2,1)} %get-tuple-element.11), channel_id=1, source_target_pairs={{0,8},{4,12},{8,0},{12,4},{1,9},{5,13},{9,1},{13,5},{2,10},{6,14},... | collective-permute-start | bytes 645128 | tf_op jit(solution)/shard_map/ppermute | solution.py:89
  5.4 16.1 %copy.6 = bf16[224,8,2,2048]{3,1,2,0:T(8,128)(2,1)} copy(bf16[224,8,2,2048]{3,2,1,0:T(2,128)(2,1)} %bitcast.36) | data formatting | bytes 29360128
  21.5 8.9 %convolution_convert_fusion = bf16[240,4096]{1,0:T(8,128)(2,1)S(1)} fusion(bf16[1792,4096]{1,0:T(8,128)(2,1)} %bitcast.37, bf16[60,1792]{1,0:T(8,128)(2,1)S(1)} %collective-permute-done.2, bf16[60,1792]{1,0:T(8,128)(2,1)S(1)} %collective-permute-done.1, bf16[60,1792]{1,0:T(8,128)(2,1)S(1)} %collective-permute-done, bf16[60,1792]{1,0:T(8,128)(2,1)S(1)} %copy-done.4), kind=kOutput, calls=%fused_computation | convolution fusion | flops 3527639040 | bytes 17506304 | tf_op jit(solution)/shard_map/dot_general | solution.py:94
  31.5 3.8 %collective-permute-start.3 = (bf16[240,1024]{1,0:T(8,128)(2,1)S(1)}, bf16[240,1024]{1,0:T(8,128)(2,1)S(1)}, u32[]{:S(2)}, u32[]{:S(2)}) collective-permute-start(bf16[240,1024]{1,0:T(8,128)(2,1)S(1)} %pad_maximum_fusion), channel_id=1, source_target_pairs={{0,1},{3,2},{4,5},{7,6},{8,9},{11,10},{12,13},{15,14},{16,17},{19,... | collective-permute-start | bytes 1474568 | tf_op jit(solution)/shard_map/ppermute | solution.py:104
  35.4 1.3 %collective-permute-start.6 = (bf16[240,1024]{1,0:T(8,128)(2,1)S(1)}, bf16[240,1024]{1,0:T(8,128)(2,1)S(1)}, u32[]{:S(2)}, u32[]{:S(2)}) collective-permute-start(bf16[240,1024]{1,0:T(8,128)(2,1)S(1)} %pad_maximum_fusion.1), channel_id=1, source_target_pairs={{0,1},{3,2},{4,5},{7,6},{8,9},{11,10},{12,13},{15,14},{16,17},{19,... | collective-permute-start | bytes 1474568 | tf_op jit(solution)/shard_map/ppermute | solution.py:104
  36.7 10.2 %collective-permute-done.3 = bf16[240,1024]{1,0:T(8,128)(2,1)S(1)} collective-permute-done((bf16[240,1024]{1,0:T(8,128)(2,1)S(1)}, bf16[240,1024]{1,0:T(8,128)(2,1)S(1)}, u32[]{:S(2)}, u32[]{:S(2)}) %collective-permute-start.3) | collective-permute-done | bytes 491552 | tf_op jit(solution)/shard_map/ppermute | solution.py:104
  47.7 9.0 %collective-permute-done.6 = bf16[240,1024]{1,0:T(8,128)(2,1)S(1)} collective-permute-done((bf16[240,1024]{1,0:T(8,128)(2,1)S(1)}, bf16[240,1024]{1,0:T(8,128)(2,1)S(1)}, u32[]{:S(2)}, u32[]{:S(2)}) %collective-permute-start.6) | collective-permute-done | bytes 491552 | tf_op jit(solution)/shard_map/ppermute | solution.py:104
  57.7 1.6 %collective-permute-start.7 = (bf16[240,1024]{1,0:T(8,128)(2,1)}, bf16[240,1024]{1,0:T(8,128)(2,1)}, u32[]{:S(2)}, u32[]{:S(2)}) collective-permute-start(bf16[240,1024]{1,0:T(8,128)(2,1)} %add_convert_fusion), channel_id=1, source_target_pairs={{1,2},{2,1},{5,6},{6,5},{9,10},{10,9},{13,14},{14,13},{17,18},{18,... | collective-permute-start | bytes 1474568 | tf_op jit(solution)/shard_map/ppermute | solution.py:104
  60.2 4.5 %collective-permute-start.5 = (bf16[240,1024]{1,0:T(8,128)(2,1)}, bf16[240,1024]{1,0:T(8,128)(2,1)}, u32[]{:S(2)}, u32[]{:S(2)}) collective-permute-start(bf16[240,1024]{1,0:T(8,128)(2,1)} %add_convert_fusion.1), channel_id=1, source_target_pairs={{0,1},{2,3},{1,0},{3,2},{4,5},{6,7},{5,4},{7,6},{8,9},{10,11},{9,8... | collective-permute-start | bytes 1474568 | tf_op jit(solution)/shard_map/ppermute | solution.py:104
  64.8 2.1 %fusion.3 = f32[240,1792]{1,0:T(8,128)S(1)} fusion(bf16[1,2048,1792]{2,1,0:T(8,128)(2,1)} %param.9, s32[]{:T(128)S(6)} %select_n.112), kind=kOutput, calls=%fused_computation.8 | convolution fusion | flops 440401920 | bytes 3555332 | tf_op jit(solution)/shard_map/dot_general | solution.py:122
  66.9 8.7 %collective-permute-done.5 = bf16[240,1024]{1,0:T(8,128)(2,1)} collective-permute-done((bf16[240,1024]{1,0:T(8,128)(2,1)}, bf16[240,1024]{1,0:T(8,128)(2,1)}, u32[]{:S(2)}, u32[]{:S(2)}) %collective-permute-start.5) | collective-permute-done | bytes 491552 | tf_op jit(solution)/shard_map/ppermute | solution.py:104
  75.6 1.5 %convert_add_fusion = f32[240,1024]{1,0:T(8,128)S(1)} fusion(bf16[240,1024]{1,0:T(8,128)(2,1)} %collective-permute-done.7, bf16[240,1024]{1,0:T(8,128)(2,1)} %collective-permute-done.5, bf16[240,512]{1,0:T(8,128)(2,1)S(1)} %copy-done, bf16[240,512]{1,0:T(8,128)(2,1)S(1)} %get-tuple-element.13), kind=kLoop, calls=%fused_computation.25 | loop fusion | flops 1966080 | bytes 2457600 | tf_op jit(solution)/shard_map/add | solution.py:116
  77.3 1.8 %collective-permute-start.8 = (bf16[240,512]{1,0:T(8,128)(2,1)S(1)}, bf16[240,512]{1,0:T(8,128)(2,1)S(1)}, u32[]{:S(2)}, u32[]{:S(2)}) collective-permute-start(bf16[240,512]{1,0:T(8,128)(2,1)S(1)} %fusion.27), channel_id=1, source_target_pairs={{0,1},{2,3},{1,0},{3,2},{4,5},{6,7},{5,4},{7,6},{8,9},{10,11},{9,8... | collective-permute-start | bytes 737288 | tf_op jit(solution)/shard_map/ppermute | solution.py:104
  79.8 2.1 %fusion.11 = f32[240,1792]{1,0:T(8,128)S(1)} fusion(bf16[240,512]{1,0:T(8,128)(2,1)S(1)} %fusion.27, bf16[1,2048,1792]{2,1,0:T(8,128)(2,1)} %param.9, s32[]{:T(128)S(6)} %select_n.105), kind=kOutput, calls=%fused_computation.16 | convolution fusion | flops 440401920 | bytes 3801092 | tf_op jit(solution)/shard_map/dot_general | solution.py:122
  81.9 1.9 %collective-permute-done.8 = bf16[240,512]{1,0:T(8,128)(2,1)S(1)} collective-permute-done((bf16[240,512]{1,0:T(8,128)(2,1)S(1)}, bf16[240,512]{1,0:T(8,128)(2,1)S(1)}, u32[]{:S(2)}, u32[]{:S(2)}) %collective-permute-start.8) | collective-permute-done | bytes 245792 | tf_op jit(solution)/shard_map/ppermute | solution.py:104
  84.5 1.3 %collective-permute-start.10 = (bf16[240,512]{1,0:T(8,128)(2,1)S(1)}, bf16[240,512]{1,0:T(8,128)(2,1)S(1)}, u32[]{:S(2)}, u32[]{:S(2)}) collective-permute-start(bf16[240,512]{1,0:T(8,128)(2,1)S(1)} %collective-permute-done.9), channel_id=1, source_target_pairs={{2,3},{1,0},{6,7},{5,4},{10,11},{9,8},{14,15},{13,12},{18,19},{17,... | collective-permute-start | bytes 737288 | tf_op jit(solution)/shard_map/ppermute | solution.py:104
  87.1 1.5 %collective-permute-start.12 = (bf16[240,512]{1,0:T(8,128)(2,1)S(1)}, bf16[240,512]{1,0:T(8,128)(2,1)S(1)}, u32[]{:S(2)}, u32[]{:S(2)}) collective-permute-start(bf16[240,512]{1,0:T(8,128)(2,1)S(1)} %collective-permute-done.11), channel_id=1, source_target_pairs={{2,3},{1,0},{6,7},{5,4},{10,11},{9,8},{14,15},{13,12},{18,19},{17,... | collective-permute-start | bytes 737288 | tf_op jit(solution)/shard_map/ppermute | solution.py:104
  89.2 5.7 %collective-permute-done.10 = bf16[240,512]{1,0:T(8,128)(2,1)S(1)} collective-permute-done((bf16[240,512]{1,0:T(8,128)(2,1)S(1)}, bf16[240,512]{1,0:T(8,128)(2,1)S(1)}, u32[]{:S(2)}, u32[]{:S(2)}) %collective-permute-start.10) | collective-permute-done | bytes 245792 | tf_op jit(solution)/shard_map/ppermute | solution.py:104
  95.5 3.3 %collective-permute-done.12 = bf16[240,512]{1,0:T(8,128)(2,1)S(1)} collective-permute-done((bf16[240,512]{1,0:T(8,128)(2,1)S(1)}, bf16[240,512]{1,0:T(8,128)(2,1)S(1)}, u32[]{:S(2)}, u32[]{:S(2)}) %collective-permute-start.12) | collective-permute-done | bytes 245792 | tf_op jit(solution)/shard_map/ppermute | solution.py:104
  100.3 1.5 %collective-permute-start.14 = (bf16[60,1792]{1,0:T(8,128)(2,1)S(1)}, bf16[60,1792]{1,0:T(8,128)(2,1)S(1)}, u32[]{:S(2)}, u32[]{:S(2)}) collective-permute-start(bf16[60,1792]{1,0:T(8,128)(2,1)S(1)} %get-tuple-element.26), channel_id=1, source_target_pairs={{0,8},{4,12},{8,0},{12,4},{1,9},{5,13},{9,1},{13,5},{2,10},{6,14},... | collective-permute-start | bytes 645128 | tf_op jit(solution)/shard_map/ppermute | solution.py:89
  102.1 6.6 %collective-permute-done.14.refs_2_ = bf16[60,1792]{1,0:T(8,128)(2,1)S(1)} collective-permute-done((bf16[60,1792]{1,0:T(8,128)(2,1)S(1)}, bf16[60,1792]{1,0:T(8,128)(2,1)S(1)}, u32[]{:S(2)}, u32[]{:S(2)}) %collective-permute-start.14) | collective-permute-done | bytes 215072 | tf_op jit(solution)/shard_map/ppermute | solution.py:89
  108.8 4.0 %collective-permute-done.15.refs_3_ = bf16[60,1792]{1,0:T(8,128)(2,1)S(1)} collective-permute-done((bf16[60,1792]{1,0:T(8,128)(2,1)S(1)}, bf16[60,1792]{1,0:T(8,128)(2,1)S(1)}, u32[]{:S(2)}, u32[]{:S(2)}) %collective-permute-start.15) | collective-permute-done | bytes 215072 | tf_op jit(solution)/shard_map/ppermute | solution.py:89
  113.4 3.4 %combine.1 = bf16[96,1792]{1,0:T(8,128)(2,1)} custom-call(s32[1]{0:T(128)} %bitcast.me_ref, s32[2,96]{1,0:T(2,128)} %bitcast.39, f32[2,96]{1,0:T(2,128)} %bitcast.40, bf16[60,1792]{1,0:T(8,128)(2,1)} %get-tuple-element.28.refs_0_, bf16[60,1792]{1,0:T(8,128)(2,1)} %copy-done.1, bf16[60,1792]{1,0:T(8,128)(2,1)} %copy-done.2, bf16[60,1792]{1,0:T(8,128)(2,1)} %copy-done.3), custom_call_target="tpu_custom_call" | custom-call | tf_op jit(solution)/shard_map/combine/pallas_call | solution.py:136
  (43 shorter events, 11.1 us)
Async XLA Ops:
  2.3 19.2 %collective-permute-start = (bf16[60,1792]{1,0:T(8,128)(2,1)}, bf16[60,1792]{1,0:T(8,128)(2,1)S(1)}, u32[]{:S(2)}, u32[]{:S(2)}) collective-permute-start(bf16[60,1792]{1,0:T(8,128)(2,1)} %get-tuple-element.10), channel_id=1, source_target_pairs={{0,4},{4,0},{8,12},{12,8},{1,5},{5,1},{9,13},{13,9},{2,6},{6,2},{1... | collective-permute-start | bytes 645128 | tf_op jit(solution)/shard_map/ppermute | solution.py:89
  2.8 18.7 %collective-permute-start.1 = (bf16[60,1792]{1,0:T(8,128)(2,1)}, bf16[60,1792]{1,0:T(8,128)(2,1)S(1)}, u32[]{:S(2)}, u32[]{:S(2)}) collective-permute-start(bf16[60,1792]{1,0:T(8,128)(2,1)} %get-tuple-element.11), channel_id=1, source_target_pairs={{0,8},{4,12},{8,0},{12,4},{1,9},{5,13},{9,1},{13,5},{2,10},{6,14},... | collective-permute-start | bytes 645128 | tf_op jit(solution)/shard_map/ppermute | solution.py:89
  5.2 16.2 %collective-permute-start.2 = (bf16[60,1792]{1,0:T(8,128)(2,1)}, bf16[60,1792]{1,0:T(8,128)(2,1)S(1)}, u32[]{:S(2)}, u32[]{:S(2)}) collective-permute-start(bf16[60,1792]{1,0:T(8,128)(2,1)} %get-tuple-element.12), channel_id=1, source_target_pairs={{0,12},{4,8},{8,4},{12,0},{1,13},{5,9},{9,5},{13,1},{2,14},{6,10},... | collective-permute-start | bytes 645128 | tf_op jit(solution)/shard_map/ppermute | solution.py:89
  5.4 16.1 %copy-start.4 = (bf16[60,1792]{1,0:T(8,128)(2,1)S(1)}, bf16[60,1792]{1,0:T(8,128)(2,1)}, u32[]{:S(2)}) copy-start(bf16[60,1792]{1,0:T(8,128)(2,1)} %get-tuple-element.9) | copy-start | bytes 645124
  31.5 15.3 %collective-permute-start.3 = (bf16[240,1024]{1,0:T(8,128)(2,1)S(1)}, bf16[240,1024]{1,0:T(8,128)(2,1)S(1)}, u32[]{:S(2)}, u32[]{:S(2)}) collective-permute-start(bf16[240,1024]{1,0:T(8,128)(2,1)S(1)} %pad_maximum_fusion), channel_id=1, source_target_pairs={{0,1},{3,2},{4,5},{7,6},{8,9},{11,10},{12,13},{15,14},{16,17},{19,... | collective-permute-start | bytes 1474568 | tf_op jit(solution)/shard_map/ppermute | solution.py:104
  35.4 21.4 %collective-permute-start.6 = (bf16[240,1024]{1,0:T(8,128)(2,1)S(1)}, bf16[240,1024]{1,0:T(8,128)(2,1)S(1)}, u32[]{:S(2)}, u32[]{:S(2)}) collective-permute-start(bf16[240,1024]{1,0:T(8,128)(2,1)S(1)} %pad_maximum_fusion.1), channel_id=1, source_target_pairs={{0,1},{3,2},{4,5},{7,6},{8,9},{11,10},{12,13},{15,14},{16,17},{19,... | collective-permute-start | bytes 1474568 | tf_op jit(solution)/shard_map/ppermute | solution.py:104
  47.0 12.2 %collective-permute-start.4 = (bf16[240,1024]{1,0:T(8,128)(2,1)S(1)}, bf16[240,1024]{1,0:T(8,128)(2,1)S(1)}, u32[]{:S(2)}, u32[]{:S(2)}) collective-permute-start(bf16[240,1024]{1,0:T(8,128)(2,1)S(1)} %add_convert_fusion.2), channel_id=1, source_target_pairs={{1,2},{2,1},{5,6},{6,5},{9,10},{10,9},{13,14},{14,13},{17,18},{18,... | collective-permute-start | bytes 1474568 | tf_op jit(solution)/shard_map/ppermute | solution.py:104
  56.7 29.1 %slice-start = ((s8[7340032]{0:T(1024)(128)(4,1)}), s8[3145728]{0:T(1024)(128)(4,1)S(1)}, s32[]{:S(2)}) async-start(s8[7340032]{0:T(1024)(128)(4,1)} %bitcast.34), calls=%async_computation | async-start | bytes 6291456
  57.7 9.3 %collective-permute-start.7 = (bf16[240,1024]{1,0:T(8,128)(2,1)}, bf16[240,1024]{1,0:T(8,128)(2,1)}, u32[]{:S(2)}, u32[]{:S(2)}) collective-permute-start(bf16[240,1024]{1,0:T(8,128)(2,1)} %add_convert_fusion), channel_id=1, source_target_pairs={{1,2},{2,1},{5,6},{6,5},{9,10},{10,9},{13,14},{14,13},{17,18},{18,... | collective-permute-start | bytes 1474568 | tf_op jit(solution)/shard_map/ppermute | solution.py:104
  60.2 15.4 %collective-permute-start.5 = (bf16[240,1024]{1,0:T(8,128)(2,1)}, bf16[240,1024]{1,0:T(8,128)(2,1)}, u32[]{:S(2)}, u32[]{:S(2)}) collective-permute-start(bf16[240,1024]{1,0:T(8,128)(2,1)} %add_convert_fusion.1), channel_id=1, source_target_pairs={{0,1},{2,3},{1,0},{3,2},{4,5},{6,7},{5,4},{7,6},{8,9},{10,11},{9,8... | collective-permute-start | bytes 1474568 | tf_op jit(solution)/shard_map/ppermute | solution.py:104
  64.8 10.8 %copy-start = (bf16[240,512]{1,0:T(8,128)(2,1)S(1)}, bf16[240,512]{1,0:T(8,128)(2,1)}, u32[]{:S(2)}) copy-start(bf16[240,512]{1,0:T(8,128)(2,1)} %get-tuple-element.24) | copy-start | bytes 737284
  75.6 10.2 %slice-start.1 = ((s8[7340032]{0:T(1024)(128)(4,1)}), s8[4194304]{0:T(1024)(128)(4,1)S(1)}, s32[]{:S(2)}) async-start(s8[7340032]{0:T(1024)(128)(4,1)} %bitcast.34), calls=%async_computation.1 | async-start | bytes 8388608
  77.3 6.5 %collective-permute-start.8 = (bf16[240,512]{1,0:T(8,128)(2,1)S(1)}, bf16[240,512]{1,0:T(8,128)(2,1)S(1)}, u32[]{:S(2)}, u32[]{:S(2)}) collective-permute-start(bf16[240,512]{1,0:T(8,128)(2,1)S(1)} %fusion.27), channel_id=1, source_target_pairs={{0,1},{2,3},{1,0},{3,2},{4,5},{6,7},{5,4},{7,6},{8,9},{10,11},{9,8... | collective-permute-start | bytes 737288 | tf_op jit(solution)/shard_map/ppermute | solution.py:104
  79.1 5.4 %collective-permute-start.9 = (bf16[240,512]{1,0:T(8,128)(2,1)S(1)}, bf16[240,512]{1,0:T(8,128)(2,1)S(1)}, u32[]{:S(2)}, u32[]{:S(2)}) collective-permute-start(bf16[240,512]{1,0:T(8,128)(2,1)S(1)} %fusion.27), channel_id=1, source_target_pairs={{1,2},{2,1},{5,6},{6,5},{9,10},{10,9},{13,14},{14,13},{17,18},{18,... | collective-permute-start | bytes 737288 | tf_op jit(solution)/shard_map/ppermute | solution.py:104
  83.8 3.3 %collective-permute-start.11 = (bf16[240,512]{1,0:T(8,128)(2,1)S(1)}, bf16[240,512]{1,0:T(8,128)(2,1)S(1)}, u32[]{:S(2)}, u32[]{:S(2)}) collective-permute-start(bf16[240,512]{1,0:T(8,128)(2,1)S(1)} %collective-permute-done.8), channel_id=1, source_target_pairs={{1,2},{2,1},{5,6},{6,5},{9,10},{10,9},{13,14},{14,13},{17,18},{18,... | collective-permute-start | bytes 737288 | tf_op jit(solution)/shard_map/ppermute | solution.py:104
  84.5 10.4 %collective-permute-start.10 = (bf16[240,512]{1,0:T(8,128)(2,1)S(1)}, bf16[240,512]{1,0:T(8,128)(2,1)S(1)}, u32[]{:S(2)}, u32[]{:S(2)}) collective-permute-start(bf16[240,512]{1,0:T(8,128)(2,1)S(1)} %collective-permute-done.9), channel_id=1, source_target_pairs={{2,3},{1,0},{6,7},{5,4},{10,11},{9,8},{14,15},{13,12},{18,19},{17,... | collective-permute-start | bytes 737288 | tf_op jit(solution)/shard_map/ppermute | solution.py:104
  87.1 11.7 %collective-permute-start.12 = (bf16[240,512]{1,0:T(8,128)(2,1)S(1)}, bf16[240,512]{1,0:T(8,128)(2,1)S(1)}, u32[]{:S(2)}, u32[]{:S(2)}) collective-permute-start(bf16[240,512]{1,0:T(8,128)(2,1)S(1)} %collective-permute-done.11), channel_id=1, source_target_pairs={{2,3},{1,0},{6,7},{5,4},{10,11},{9,8},{14,15},{13,12},{18,19},{17,... | collective-permute-start | bytes 737288 | tf_op jit(solution)/shard_map/ppermute | solution.py:104
  100.3 1.9 %collective-permute-start.13 = (bf16[60,1792]{1,0:T(8,128)(2,1)S(1)}, bf16[60,1792]{1,0:T(8,128)(2,1)S(1)}, u32[]{:S(2)}, u32[]{:S(2)}) collective-permute-start(bf16[60,1792]{1,0:T(8,128)(2,1)S(1)} %get-tuple-element.27), channel_id=1, source_target_pairs={{0,4},{4,0},{8,12},{12,8},{1,5},{5,1},{9,13},{13,9},{2,6},{6,2},{1... | collective-permute-start | bytes 645128 | tf_op jit(solution)/shard_map/ppermute | solution.py:89
  100.3 8.5 %collective-permute-start.14 = (bf16[60,1792]{1,0:T(8,128)(2,1)S(1)}, bf16[60,1792]{1,0:T(8,128)(2,1)S(1)}, u32[]{:S(2)}, u32[]{:S(2)}) collective-permute-start(bf16[60,1792]{1,0:T(8,128)(2,1)S(1)} %get-tuple-element.26), channel_id=1, source_target_pairs={{0,8},{4,12},{8,0},{12,4},{1,9},{5,13},{9,1},{13,5},{2,10},{6,14},... | collective-permute-start | bytes 645128 | tf_op jit(solution)/shard_map/ppermute | solution.py:89
  101.8 11.0 %collective-permute-start.15 = (bf16[60,1792]{1,0:T(8,128)(2,1)S(1)}, bf16[60,1792]{1,0:T(8,128)(2,1)S(1)}, u32[]{:S(2)}, u32[]{:S(2)}) collective-permute-start(bf16[60,1792]{1,0:T(8,128)(2,1)S(1)} %get-tuple-element.25), channel_id=1, source_target_pairs={{0,12},{4,8},{8,4},{12,0},{1,13},{5,9},{9,5},{13,1},{2,14},{6,10},... | collective-permute-start | bytes 645128 | tf_op jit(solution)/shard_map/ppermute | solution.py:89
  102.1 10.6 %copy-start.1 = (bf16[60,1792]{1,0:T(8,128)(2,1)}, bf16[60,1792]{1,0:T(8,128)(2,1)S(1)}, u32[]{:S(2)}) copy-start(bf16[60,1792]{1,0:T(8,128)(2,1)S(1)} %collective-permute-done.13.refs_1_) | copy-start | bytes 645124
  108.8 4.0 %copy-start.2 = (bf16[60,1792]{1,0:T(8,128)(2,1)}, bf16[60,1792]{1,0:T(8,128)(2,1)S(1)}, u32[]{:S(2)}) copy-start(bf16[60,1792]{1,0:T(8,128)(2,1)S(1)} %collective-permute-done.14.refs_2_) | copy-start | bytes 645124
  112.8 0.7 copy-start.3

commit v2 on v0

v2 whole, which is shorter than its diff:
```python
import functools

import jax
import jax.numpy as jnp
from jax import lax
from jax.experimental import pallas as pl
from jax.experimental.pallas import tpu as pltpu
from jax.sharding import PartitionSpec as P

F32, BF16, I32 = jnp.float32, jnp.bfloat16, jnp.int32
LANES = 128
PARTS = 1


def batches(capacity):
    step = -(-capacity // PARTS)
    step = min(capacity, -(-step // 16) * 16) if PARTS > 1 else capacity
    return [(first, min(step, capacity - first)) for first in range(0, capacity, step)]


def block_to_send(here, replicas, step, parity):
    right, left = replicas - step + here, here - replicas + step
    return jnp.clip(jnp.where(here % 2 == parity, right, left), 0, replicas - 1)


def paired(here, replicas, parity):
    other = jnp.where(here % 2 == parity, here + 1, here - 1)
    return (other >= 0) & (other < replicas)


def block_in_order(here, replicas, t):
    return (block_to_send(here, replicas, 1, 0) + t) % replicas


def dispatch_body(me_ref, ids_hbm, tokens_hbm, *refs, experts, runs):
    *out_refs, ids_ref, tokens_ref, done = refs
    ids_copy = pltpu.make_async_copy(ids_hbm, ids_ref, done.at[0])
    tokens_copy = pltpu.make_async_copy(tokens_hbm, tokens_ref, done.at[1])
    ids_copy.start()
    tokens_copy.start()
    ids_copy.wait()
    ids = ids_ref[...]
    choices, rows = ids.shape
    label = me_ref[0] ^ lax.broadcasted_iota(I32, (experts, rows), 0)
    chosen = jnp.zeros((experts, rows), F32)
    for k in range(choices):
        chosen = chosen + (ids[k : k + 1] == label).astype(F32)
    earlier = lax.broadcasted_iota(I32, (rows, rows), 0) < lax.broadcasted_iota(I32, (rows, rows), 1)
    rank = jnp.dot(chosen.astype(BF16), earlier.astype(F32).astype(BF16), preferred_element_type=F32)
    slot = jnp.where(chosen > 0, rank.astype(I32), -1)
    tokens_copy.wait()
    tokens = tokens_ref[...]
    for b, (first, count) in enumerate(runs):
        for s in range(experts):
            pick = slot[s : s + 1] == first + lax.broadcasted_iota(I32, (count, rows), 0)
            pick = pick.astype(F32).astype(BF16)
            out_refs[b * experts + s][...] = jnp.dot(pick, tokens, preferred_element_type=F32).astype(BF16)


def mixing_body(me_ref, ids_ref, affinity_ref, out_ref, *, experts, runs):
    ids, affinity = ids_ref[...], affinity_ref[...]
    rows, choices = ids.shape
    label = me_ref[0] ^ lax.broadcasted_iota(I32, (rows, experts), 1)
    chosen = jnp.zeros((rows, experts), F32)
    for k in range(choices):
        chosen = chosen + (ids[:, k : k + 1] == label).astype(F32)
    earlier = lax.broadcasted_iota(I32, (rows, rows), 1) < lax.broadcasted_iota(I32, (rows, rows), 0)
    rank = jnp.dot(earlier.astype(F32).astype(BF16), chosen.astype(BF16), preferred_element_type=F32)
    weights = 2.5 * affinity / jnp.sum(affinity, axis=1, keepdims=True)
    base = 0
    for first, count in runs:
        padded = -(-count // 16) * 16
        within = rank.astype(I32) - first
        place = base + padded * lax.broadcasted_iota(I32, (rows, experts), 1) + within
        place = jnp.where((chosen > 0) & (within >= 0) & (within < count), place, -1)
        column = base + lax.broadcasted_iota(I32, (rows, experts * padded), 1)
        rest = jnp.zeros(column.shape, F32)
        for k in range(choices):
            mine = ids[:, k : k + 1] == label
            spot = jnp.max(jnp.where(mine, place, -1), axis=1, keepdims=True)
            rest = rest + jnp.where(spot == column, weights[:, k : k + 1], 0.0)
        for i in range(3):
            part = rest.astype(BF16)
            rest = rest - part.astype(F32)
            out_ref[i, :, base : base + experts * padded] = part
        base += experts * padded


def combine_body(mixing_ref, *refs, runs, experts):
    *in_refs, out, gathered = refs
    base = 0
    for b, (first, count) in enumerate(runs):
        padded = -(-count // 16) * 16
        for s in range(experts):
            if padded > count:
                tail = base + padded - 16
                gathered[tail : tail + 16] = jnp.zeros((16, gathered.shape[1]), BF16)
            gathered[base : base + count] = in_refs[b * experts + s][...]
            base += padded
    rows = out.shape[0]
    terms, _, slots = mixing_ref.shape
    picked = jnp.dot(
        mixing_ref[...].reshape(terms * rows, slots), gathered[...], preferred_element_type=F32
    )
    total = picked[:rows]
    for i in range(1, terms):
        total = total + picked[i * rows : (i + 1) * rows]
    out[...] = total.astype(BF16)


def tile_copy(pairs_ref, tile, buffer_ref, at, done):
    return pltpu.make_async_copy(pairs_ref.at[:, tile], buffer_ref.at[at], done.at[at])


def prepare_body(place_ref, *refs, replicas, start):
    pairs_ref, out_ref, buffer_ref, done = refs[-4:]
    blocks, width, columns = out_ref.shape
    per = columns // (2 * LANES)
    pairs_per = per // 2
    steps = blocks * pairs_per
    depth = buffer_ref.shape[0] // 2
    flat = buffer_ref.reshape(2 * depth, 2 * width, LANES)

    def fetch(t):
        q = block_in_order(place_ref[1], replicas, start + t // pairs_per)
        tile = q * per + 2 * (t % pairs_per)
        for i in range(2):
            tile_copy(pairs_ref, tile + i, buffer_ref, 2 * (t % depth) + i, done).start()

    for t in range(min(depth - 1, steps)):
        fetch(t)
    side = 2 * LANES
    row = lax.broadcasted_iota(I32, (side, side), 0)
    column = lax.broadcasted_iota(I32, (side, side), 1)
    sort = (column == 2 * row) | (column == 2 * (row - LANES) + 1)
    sort = sort.astype(F32).astype(BF16)

    def step(t, carry):
        @pl.when(t + depth - 1 < steps)
        def _():
            fetch(t + depth - 1)

        q = t // pairs_per
        gate = pl.multiple_of((t % pairs_per) * side, side)
        up = pl.multiple_of(per * LANES + (t % pairs_per) * side, side)
        at = 2 * (t % depth)
        for i in range(2):
            tile_copy(pairs_ref, 0, buffer_ref, at + i, done).wait()
        for r in range(width // LANES):
            rows = slice(r * side, (r + 1) * side)
            mixed = jnp.concatenate([flat[at, rows], flat[at + 1, rows]], axis=1)
            sorted_rows = jnp.dot(sort, mixed, preferred_element_type=F32).astype(BF16)
            out_ref[q, r * LANES : (r + 1) * LANES, pl.ds(gate, side)] = sorted_rows[:LANES]
            out_ref[q, r * LANES : (r + 1) * LANES, pl.ds(up, side)] = sorted_rows[LANES:]
        return carry

    lax.fori_loop(0, steps, step, 0)


def gather_rows(x_refs, rows_ref):
    count = rows_ref.shape[0] // len(x_refs)
    for s, x in enumerate(x_refs):
        rows_ref[s * count : (s + 1) * count] = x[...]


def columns_of(rows_ref, weights_ref, t, store):
    for c in range(0, weights_ref.shape[2], 2 * LANES):
        part = weights_ref[t, :, c : c + 2 * LANES]
        store(c, jnp.dot(rows_ref[...], part, preferred_element_type=F32).astype(BF16))


def first_body(*refs, experts):
    x_refs, (weights_ref, first_ref, rows_ref) = refs[:experts], refs[experts:]
    gather_rows(x_refs, rows_ref)

    def store(c, value):
        first_ref[:, c : c + 2 * LANES] = value

    columns_of(rows_ref, weights_ref, 0, store)


def rest_body(place_ref, first_ref, *refs, experts):
    x_refs, (early_ref, late_ref, out_ref, second_ref, rows_ref) = refs[:experts], refs[experts:]
    here, blocks = place_ref[1], out_ref.shape[0]
    gather_rows(x_refs, rows_ref)
    out_ref[block_in_order(here, blocks, 0)] = first_ref[...]
    for t in range(1, blocks):
        q = block_in_order(here, blocks, t)

        def store(c, value):
            out_ref[q, :, c : c + 2 * LANES] = value

        early = early_ref.shape[0]
        columns_of(rows_ref, early_ref if t < early else late_ref, t if t < early else t - early, store)
    second_ref[...] = out_ref[block_to_send(here, blocks, 2, 0)]


def add_body(place_ref, partial_ref, got_ref, out_ref, *, step, parity):
    here, replicas = place_ref[1], partial_ref.shape[0]
    own = partial_ref[block_to_send(here, replicas, step, parity)].astype(F32)
    got = jnp.where(paired(here, replicas, 1 - parity), got_ref[...].astype(F32), 0.0)
    out_ref[...] = (own + got).astype(BF16)


def hidden_body(place_ref, partial_ref, *refs, parities):
    *got_refs, out_ref = refs
    here, replicas = place_ref[1], partial_ref.shape[0]
    pre = partial_ref[here].astype(F32)
    for parity, got in zip(parities, got_refs):
        pre = pre + jnp.where(paired(here, replicas, parity), got[...].astype(F32), 0.0)
    block = out_ref.shape[1]
    gate = pre[:, :block]
    out_ref[...] = (gate / (1.0 + jnp.exp(-gate)) * pre[:, block:]).astype(BF16)


def down_body(place_ref, down_ref, *refs, step, parities, own, last, replicas):
    here = place_ref[1]
    block = down_ref.shape[0] // replicas
    known = refs[0]
    got_refs = refs[1 : 1 + len(parities)]
    out_refs = refs[1 + len(parities) :]
    total = out_refs[-1]

    def product(h_ref, q):
        part = down_ref[pl.ds(pl.multiple_of(q * block, block), block)]
        return jnp.dot(h_ref[...], part, preferred_element_type=F32)

    total[...] = product(known, here) if own else known[...]
    for parity, got in zip(parities, got_refs):
        q = jnp.where(here % 2 == parity, here + step, here - step)

        @pl.when((q >= 0) & (q < replicas))
        def _():
            total[...] = total[...] + product(got, q)

    if last:
        count = out_refs[0].shape[0]
        for s, out in enumerate(out_refs[:-1]):
            out[...] = total[s * count : (s + 1) * count].astype(BF16)


def vmem(count):
    return [pl.BlockSpec(memory_space=pltpu.VMEM)] * count


def smem():
    return [pl.BlockSpec(memory_space=pltpu.SMEM)]


def hbm(count):
    return [pl.BlockSpec(memory_space=pltpu.HBM)] * count


def in_hbm(x):
    return pltpu.with_memory_space_constraint(x, pltpu.HBM)


def params(mib):
    return pltpu.CompilerParams(vmem_limit_bytes=mib << 20)


def partner(p, parity):
    return p + 1 if p % 2 == parity else p - 1


def neighbours(experts, count, parity):
    swaps = []
    for e in range(experts):
        for p in range(count):
            q = partner(p, parity)
            other = (e, q) if 0 <= q < count else (e ^ 1, p)
            swaps.append((e * count + p, other[0] * count + other[1]))
    return swaps


def needed(count, parity, right, left):
    edges = [p for p in range(count - 1) if p % 2 == parity]
    return any(right(p) or left(p + 1) for p in edges)


def per_device(tokens, expert_ids, affinity, gate_up, down_proj):
    experts, replicas = lax.axis_size("expert"), lax.axis_size("replica")
    rows, choices = expert_ids.shape
    capacity = 5 * rows * choices // (4 * experts)
    runs = batches(capacity)
    width = tokens.shape[1]
    hidden_width = down_proj.shape[1]
    block = hidden_width // replicas
    me = lax.axis_index("expert").astype(I32)[None]
    here = lax.axis_index("replica").astype(I32)
    place = jnp.stack([me[0], here])

    slots = pl.pallas_call(
        functools.partial(dispatch_body, experts=experts, runs=runs),
        out_shape=[jax.ShapeDtypeStruct((c, width), BF16) for _, c in runs for _ in range(experts)],
        in_specs=smem() + hbm(2),
        out_specs=vmem(experts * len(runs)),
        scratch_shapes=[
            pltpu.VMEM((choices, rows), I32),
            pltpu.VMEM((rows, width), BF16),
            pltpu.SemaphoreType.DMA((2,)),
        ],
        compiler_params=params(8),
        name="dispatch",
    )(place, in_hbm(expert_ids.T), in_hbm(tokens))

    def swap(x, s):
        return lax.ppermute(x, "expert", [(i, i ^ s) for i in range(experts)])

    def hop(x, parity):
        return lax.ppermute(x, ("expert", "replica"), neighbours(experts, replicas, parity))

    arrived = []
    for b in range(len(runs)):
        mine = slots[b * experts : (b + 1) * experts]
        far_first = {s: swap(mine[s], s) for s in range(experts - 1, 0, -1)}
        arrived.append([mine[0]] + [far_first[s] for s in range(1, experts)])

    tiles = hidden_width // LANES
    pairs = gate_up[0].reshape(width, 2, tiles, LANES).transpose(0, 2, 1, 3)
    pairs = in_hbm(pairs)

    def tile_buffers(count):
        return [pltpu.VMEM((count, width, 2, LANES), BF16), pltpu.SemaphoreType.DMA((count,))]

    slots_padded = sum(experts * (-(-c // 16) * 16) for _, c in runs)
    mixing = pl.pallas_call(
        functools.partial(mixing_body, experts=experts, runs=runs),
        out_shape=jax.ShapeDtypeStruct((3, rows, slots_padded), BF16),
        in_specs=smem() + vmem(2),
        out_specs=vmem(1)[0],
        compiler_params=params(8),
        name="mixing",
    )(place, expert_ids, affinity)

    def prepared(start, count, *after):
        return pl.pallas_call(
            functools.partial(prepare_body, replicas=replicas, start=start),
            out_shape=jax.ShapeDtypeStruct((count, width, 2 * block), BF16),
            in_specs=smem() + hbm(1 + len(after)),
            out_specs=vmem(1)[0],
            scratch_shapes=tile_buffers(8),
            compiler_params=params(12),
            name="prepare",
        )(place, *after, pairs)

    early = replicas - replicas // 4
    weights = prepared(0, early)

    def first(x):
        return pl.pallas_call(
            functools.partial(first_body, experts=experts),
            out_shape=jax.ShapeDtypeStruct((experts * x[0].shape[0], 2 * block), BF16),
            in_specs=vmem(experts + 1),
            out_specs=vmem(1)[0],
            scratch_shapes=[pltpu.VMEM((experts * x[0].shape[0], width), BF16)],
            compiler_params=params(8),
            name="first",
        )(*x, weights)

    def reduced(x, ahead, late):
        count = experts * x[0].shape[0]
        sent = jax.ShapeDtypeStruct((count, 2 * block), BF16)
        partial, second = pl.pallas_call(
            functools.partial(rest_body, experts=experts),
            out_shape=[jax.ShapeDtypeStruct((replicas, count, 2 * block), BF16), sent],
            in_specs=smem() + vmem(3 + experts),
            out_specs=vmem(2),
            scratch_shapes=[pltpu.VMEM((count, width), BF16)],
            compiler_params=params(8),
            name="rest",
        )(place, ahead, *x, weights, late)

        def added(step, parity, got):
            return pl.pallas_call(
                functools.partial(add_body, step=step, parity=parity),
                out_shape=sent,
                in_specs=smem() + vmem(2),
                out_specs=vmem(1)[0],
                compiler_params=params(4),
                name="add",
            )(place, partial, got)

        got = [None, None]
        for s in range(1, replicas):
            right, left = (lambda p: p <= s - 1), (lambda p: p >= replicas - s)
            came = list(got)
            for parity in range(2):
                if not needed(replicas, parity, right, left):
                    continue
                if came[1 - parity] is not None:
                    send = added(s, parity, came[1 - parity])
                elif parity == 0 and s <= 2:
                    send = (ahead, second)[s - 1]
                else:
                    q = block_to_send(here, replicas, s, parity)
                    send = lax.dynamic_index_in_dim(partial, q, 0, keepdims=False)
                got[parity] = hop(send, parity)
        parities = [parity for parity in range(2) if got[parity] is not None]
        return pl.pallas_call(
            functools.partial(hidden_body, parities=parities),
            out_shape=jax.ShapeDtypeStruct((count, block), BF16),
            in_specs=smem() + vmem(1 + len(parities)),
            out_specs=vmem(1)[0],
            compiler_params=params(4),
            name="hidden",
        )(place, partial, *[got[parity] for parity in parities])

    def projected(hidden):
        count = hidden.shape[0]
        send, known = [hidden, hidden], hidden
        for s in range(1, replicas):
            right, left = (lambda p: p >= s - 1), (lambda p: p <= replicas - s)
            got = [None, None]
            for parity in range(2):
                if needed(replicas, parity, right, left):
                    got[parity] = hop(send[parity], parity)
            parities = [parity for parity in range(2) if got[parity] is not None]
            last = s == replicas - 1
            back = [jax.ShapeDtypeStruct((count // experts, width), BF16)] * (experts if last else 0)
            *back, known = pl.pallas_call(
                functools.partial(
                    down_body, step=s, parities=parities, own=s == 1, last=last, replicas=replicas
                ),
                out_shape=[*back, jax.ShapeDtypeStruct((count, width), F32)],
                in_specs=smem() + vmem(2 + len(parities)),
                out_specs=vmem(len(back) + 1),
                input_output_aliases={} if s == 1 else {2: len(back)},
                compiler_params=params(8),
                name="down",
            )(place, down_proj[0], known, *[got[parity] for parity in parities])
            send = got[::-1]
        far_first = {s: swap(back[s], s) for s in range(experts - 1, 0, -1)}
        return [back[0]] + [far_first[s] for s in range(1, experts)]

    ahead = [first(x) for x in arrived]
    late = prepared(early, replicas - early, in_hbm(ahead[0]))
    hidden = [reduced(x, a, late) for x, a in zip(arrived, ahead)]
    returned = [r for h in hidden for r in projected(h)]
    return pl.pallas_call(
        functools.partial(combine_body, runs=runs, experts=experts),
        out_shape=jax.ShapeDtypeStruct((rows, width), BF16),
        in_specs=vmem(1 + len(returned)),
        out_specs=vmem(1)[0],
        scratch_shapes=[pltpu.VMEM((slots_padded, width), BF16)],
        compiler_params=params(16),
        name="combine",
    )(mixing, *returned)


def solution(mesh):
    placed = (
        P(("groups", "expert"), "replica"),
        P(("groups", "expert"), None),
        P(("groups", "expert"), None),
        P("expert", "replica", None, None),
        P("expert", None, "replica"),
    )
    return jax.shard_map(
        per_device,
        mesh=mesh,
        in_specs=placed,
        out_specs=P(("groups", "expert"), "replica"),
        check_vma=False,
    )
```

time: 177 us -> 92.8 us (0.52)
  waiting for transfers between devices: 101 us -> 38.8 us
  Pallas kernels: 0 us -> 31.3 us
  local copies, waits for them, and re-layouts: 32.4 us -> 1.26 us
  matrix products: 16.2 us -> 0 us
  between operations: 13.6 us -> 0.21 us
  starting transfers between devices: 7.74 us -> 21 us
  other arithmetic: 5.03 us -> 0.08 us
    psum x1 -> x0, waiting for transfers between devices: 88.8 us -> none  [per_device(): summed = lax.psum(partial_rows, 'replica').astype(jnp.float32)]
    ppermute x0 -> x16, waiting for transfers between devices: none -> 38.8 us  [the longest x10 28.7 us: hop(): lax.ppermute(x, ('expert', 'replica'), neighbours(experts, replicas, pari...]
    pallas_call x0 -> x14, Pallas kernels: none -> 31.3 us  [the longest x2 15 us: prepared(): pl.pallas_call(functools.partial(prepare_body, replicas=replicas, start=s...]
    ppermute x0 -> x16, starting transfers between devices: none -> 21 us  [the longest x10 16 us: hop(): lax.ppermute(x, ('expert', 'replica'), neighbours(experts, replicas, pari...]
    dot_general x3 -> x0, matrix products: 16.2 us -> none  [the longest x1 10.3 us: per_device(): jnp.dot(slot_block.reshape(group_count * item_count, feature_count), pair...]
    unnamed x3 -> x14, local copies, waits for them, and re-layouts: 16.1 us -> 1.26 us
    all_to_all x2 -> x0, waiting for transfers between devices: 12.6 us -> none  [the longest x1 12.6 us: per_device(): lax.all_to_all(expert_rows, 'expert', split_axis=0, concat_axis=0, tiled=...]
    reshape x8 -> x0, local copies, waits for them, and re-layouts: 9.74 us -> none  [the longest x2 6.97 us: per_device(): partial_sum.astype(jnp.bfloat16)]
  transfers between devices with their start and end apart: 3 -> 16, of which waited for: 2 -> 8; matrix products, arithmetic and copies ran while one was open for 9% -> 0% of each run, Pallas kernels for 0% -> 27%
where the time goes in v2:
time: 92.8 us; the launch traced here: 92.6 us
  waiting for transfers between devices  38.8 us (42%)
  Pallas kernels  31.3 us (34%)
  starting transfers between devices  21 us (23%)
  local copies, waits for them, and re-layouts  1.26 us (1%)
    ppermute x10, waiting for transfers between devices, hop(): lax.ppermute(x, ('expert', 'replica'), neighbours(experts, replicas, pari...  28.7 us
    ppermute x10, starting transfers between devices, hop(): lax.ppermute(x, ('expert', 'replica'), neighbours(experts, replicas, pari...  16 us
    pallas_call x2, Pallas kernels, prepared(): pl.pallas_call(functools.partial(prepare_body, replicas=replicas, start=s...  15 us
    ppermute x6, waiting for transfers between devices, swap(): return lax.ppermute(x, 'expert', [(i, i ^ s) for i in range(experts)])  10.1 us
    ppermute x6, starting transfers between devices, swap(): return lax.ppermute(x, 'expert', [(i, i ^ s) for i in range(experts)])  5.07 us
    pallas_call x3, Pallas kernels, projected(): pl.pallas_call(functools.partial(down_body, step=s, parities=parities, ow...  4.64 us
    pallas_call x1, Pallas kernels, reduced(): pl.pallas_call(functools.partial(rest_body, experts=experts), out_shape=[...  3.46 us
    pallas_call x3, Pallas kernels, added(): pl.pallas_call(functools.partial(add_body, step=step, parity=parity), out...  2.1 us
  transfers between devices with their start and end apart: 16, of which 8 were waited for; matrix products, arithmetic and copies ran while one was open for 0% of the time, Pallas kernels for 27%

profile of v2, /device:TPU:0, one launch (start us, length us, event | category | flops | bytes accessed | tf_op | source)
XLA Modules:
  0.0 92.6 jit_solution(15395675694585890141)
XLA Ops:
  0.1 1.9 %dispatch.1 = (bf16[60,1792]{1,0:T(8,128)(2,1)S(1)}, bf16[60,1792]{1,0:T(8,128)(2,1)S(1)}, bf16[60,1792]{1,0:T(8,128)(2,1)S(1)}, bf16[60,1792]{1,0:T(8,128)(2,1)S(1)}) custom-call(s32[2]{0:T(128)S(1)} %pad_add_fusion.me_ref.place_ref, s32[2,96]{1,0:T(2,128)} %bitcast.14, bf16[96,1792]{1,0:T(8,128)(2,1)} %tokens_hbm.1), custom_call_target="tpu_custom_call" | custom-call | tf_op jit(solution)/shard_map/dispatch/pallas_call | solution.py:293
  2.6 2.5 %collective-permute-start.1 = (bf16[60,1792]{1,0:T(8,128)(2,1)S(1)}, bf16[60,1792]{1,0:T(8,128)(2,1)S(1)}, u32[]{:S(2)}, u32[]{:S(2)}) collective-permute-start(bf16[60,1792]{1,0:T(8,128)(2,1)S(1)} %get-tuple-element.17), channel_id=1, source_target_pairs={{0,8},{4,12},{8,0},{12,4},{1,9},{5,13},{9,1},{13,5},{2,10},{6,14},... | collective-permute-start | bytes 645128 | tf_op jit(solution)/shard_map/ppermute | solution.py:308
  5.2 10.0 %prepare.2.refs_4_ = bf16[3,1792,1024]{2,1,0:T(8,128)(2,1)S(1)} custom-call(s32[2]{0:T(128)S(1)} %pad_add_fusion.me_ref.place_ref, bf16[1792,16,2,128]{3,2,1,0:T(2,128)(2,1)} %bitcast.12), custom_call_target="tpu_custom_call" | custom-call | tf_op jit(solution)/shard_map/prepare/pallas_call | solution.py:337
  16.0 1.1 %first.1.refs_0_.first_ref = bf16[240,1024]{1,0:T(8,128)(2,1)S(1)} custom-call(bf16[60,1792]{1,0:T(8,128)(2,1)S(1)} %get-tuple-element.15.refs_0_, bf16[60,1792]{1,0:T(8,128)(2,1)S(1)} %collective-permute-done.refs_1_, bf16[60,1792]{1,0:T(8,128)(2,1)S(1)} %collective-permute-done.1.refs_2_, bf16[60,1792]{1,0:T(8,128)(2,1)S(1)} %collective-permute-done.2.refs_3_, ...), custom_call_target="tpu_custom_call" | custom-call | tf_op jit(solution)/shard_map/first/pallas_call | solution.py:351
  17.1 1.6 %collective-permute-start.3 = (bf16[240,1024]{1,0:T(8,128)(2,1)S(1)}, bf16[240,1024]{1,0:T(8,128)(2,1)S(1)}, u32[]{:S(2)}, u32[]{:S(2)}) collective-permute-start(bf16[240,1024]{1,0:T(8,128)(2,1)S(1)} %first.1.refs_0_.first_ref), channel_id=1, source_target_pairs={{0,1},{1,0},{2,3},{3,2},{4,5},{5,4},{6,7},{7,6},{8,9},{9,8},{10,11... | collective-permute-start | bytes 1474568 | tf_op jit(solution)/shard_map/ppermute | solution.py:311
  18.7 5.0 %prepare.3.refs_5_ = bf16[1,1792,1024]{2,1,0:T(8,128)(2,1)S(1)} custom-call(s32[2]{0:T(128)S(1)} %pad_add_fusion.me_ref.place_ref, bf16[240,1024]{1,0:T(8,128)(2,1)} %copy-done, bf16[1792,16,2,128]{3,2,1,0:T(2,128)(2,1)} %bitcast.13), custom_call_target="tpu_custom_call" | custom-call | tf_op jit(solution)/shard_map/prepare/pallas_call | solution.py:337
  23.7 1.0 %copy-done.1 = bf16[240,1024]{1,0:T(8,128)(2,1)S(1)} copy-done((bf16[240,1024]{1,0:T(8,128)(2,1)S(1)}, bf16[240,1024]{1,0:T(8,128)(2,1)}, u32[]{:S(2)}) %copy-start.1) | copy-done | bytes 491544
  24.7 3.5 %rest.1 = (bf16[4,240,1024]{2,1,0:T(8,128)(2,1)S(1)}, bf16[240,1024]{1,0:T(8,128)(2,1)S(1)}) custom-call(s32[2]{0:T(128)S(1)} %pad_add_fusion.me_ref.place_ref, bf16[240,1024]{1,0:T(8,128)(2,1)S(1)} %copy-done.1, bf16[60,1792]{1,0:T(8,128)(2,1)S(1)} %get-tuple-element.15.refs_0_, bf16[60,1792]{1,0:T(8,128)(2,1)S(1)} %collective-permute-done.refs_1_, ...), custom_call_target="tpu_custom_call" | custom-call | tf_op jit(solution)/shard_map/rest/pallas_call | solution.py:364
  29.0 1.4 %collective-permute-done.3.got_ref = bf16[240,1024]{1,0:T(8,128)(2,1)S(1)} collective-permute-done((bf16[240,1024]{1,0:T(8,128)(2,1)S(1)}, bf16[240,1024]{1,0:T(8,128)(2,1)S(1)}, u32[]{:S(2)}, u32[]{:S(2)}) %collective-permute-start.3) | collective-permute-done | bytes 491552 | tf_op jit(solution)/shard_map/ppermute | solution.py:311
  31.2 10.3 %collective-permute-done.6.got_ref = bf16[240,1024]{1,0:T(8,128)(2,1)S(1)} collective-permute-done((bf16[240,1024]{1,0:T(8,128)(2,1)S(1)}, bf16[240,1024]{1,0:T(8,128)(2,1)S(1)}, u32[]{:S(2)}, u32[]{:S(2)}) %collective-permute-start.6) | collective-permute-done | bytes 491552 | tf_op jit(solution)/shard_map/ppermute | solution.py:311
  43.0 3.4 %collective-permute-start.5 = (bf16[240,1024]{1,0:T(8,128)(2,1)S(1)}, bf16[240,1024]{1,0:T(8,128)(2,1)S(1)}, u32[]{:S(2)}, u32[]{:S(2)}) collective-permute-start(bf16[240,1024]{1,0:T(8,128)(2,1)S(1)} %add.6), channel_id=1, source_target_pairs={{0,1},{1,0},{2,3},{3,2},{4,5},{5,4},{6,7},{7,6},{8,9},{9,8},{10,11... | collective-permute-start | bytes 1474568 | tf_op jit(solution)/shard_map/ppermute | solution.py:311
  46.4 10.3 %collective-permute-done.5.refs_0_ = bf16[240,1024]{1,0:T(8,128)(2,1)S(1)} collective-permute-done((bf16[240,1024]{1,0:T(8,128)(2,1)S(1)}, bf16[240,1024]{1,0:T(8,128)(2,1)S(1)}, u32[]{:S(2)}, u32[]{:S(2)}) %collective-permute-start.5) | collective-permute-done | bytes 491552 | tf_op jit(solution)/shard_map/ppermute | solution.py:311
  57.6 1.6 %collective-permute-start.8 = (bf16[240,512]{1,0:T(8,128)(2,1)S(1)}, bf16[240,512]{1,0:T(8,128)(2,1)S(1)}, u32[]{:S(2)}, u32[]{:S(2)}) collective-permute-start(bf16[240,512]{1,0:T(8,128)(2,1)S(1)} %hidden.1.refs_0_), channel_id=1, source_target_pairs={{0,1},{1,0},{2,3},{3,2},{4,5},{5,4},{6,7},{7,6},{8,9},{9,8},{10,11... | collective-permute-start | bytes 737288 | tf_op jit(solution)/shard_map/ppermute | solution.py:311
  59.2 4.6 %collective-permute-done.8.refs_1_ = bf16[240,512]{1,0:T(8,128)(2,1)S(1)} collective-permute-done((bf16[240,512]{1,0:T(8,128)(2,1)S(1)}, bf16[240,512]{1,0:T(8,128)(2,1)S(1)}, u32[]{:S(2)}, u32[]{:S(2)}) %collective-permute-start.8) | collective-permute-done | bytes 245792 | tf_op jit(solution)/shard_map/ppermute | solution.py:311
  63.8 4.1 %collective-permute-start.10 = (bf16[240,512]{1,0:T(8,128)(2,1)S(1)}, bf16[240,512]{1,0:T(8,128)(2,1)S(1)}, u32[]{:S(2)}, u32[]{:S(2)}) collective-permute-start(bf16[240,512]{1,0:T(8,128)(2,1)S(1)} %collective-permute-done.9.refs_2_), channel_id=1, source_target_pairs={{0,1},{1,0},{2,3},{3,2},{4,5},{5,4},{6,7},{7,6},{8,9},{9,8},{10,11... | collective-permute-start | bytes 737288 | tf_op jit(solution)/shard_map/ppermute | solution.py:311
  68.0 4.3 %collective-permute-start.12 = (bf16[240,512]{1,0:T(8,128)(2,1)S(1)}, bf16[240,512]{1,0:T(8,128)(2,1)S(1)}, u32[]{:S(2)}, u32[]{:S(2)}) collective-permute-start(bf16[240,512]{1,0:T(8,128)(2,1)S(1)} %collective-permute-done.11.refs_2_), channel_id=1, source_target_pairs={{0,1},{1,0},{2,3},{3,2},{4,5},{5,4},{6,7},{7,6},{8,9},{9,8},{10,11... | collective-permute-start | bytes 737288 | tf_op jit(solution)/shard_map/ppermute | solution.py:311
  72.2 1.8 %down.3.refs_0_ = f32[240,1792]{1,0:T(8,128)S(1)} custom-call(s32[2]{0:T(128)S(1)} %pad_add_fusion.me_ref.place_ref, bf16[2048,1792]{1,0:T(8,128)(2,1)S(1)} %bitcast.9, bf16[240,512]{1,0:T(8,128)(2,1)S(1)} %hidden.1.refs_0_, bf16[240,512]{1,0:T(8,128)(2,1)S(1)} %collective-permute-done.8.refs_1_, bf16[240,512]{1,0:T(8,128)(2,1)S(1)} %collective-permute-done.9.refs_2_), custom_call_target="tpu_custom_call" | custom-call | tf_op jit(solution)/shard_map/down/pallas_call | solution.py:421
  74.0 1.4 %down.4.refs_0_ = f32[240,1792]{1,0:T(8,128)S(1)} custom-call(s32[2]{0:T(128)S(1)} %pad_add_fusion.me_ref.place_ref, bf16[2048,1792]{1,0:T(8,128)(2,1)S(1)} %bitcast.10, f32[240,1792]{1,0:T(8,128)S(1)} %down.3.refs_0_, bf16[240,512]{1,0:T(8,128)(2,1)S(1)} %collective-permute-done.10.refs_1_, ...), custom_call_target="tpu_custom_call", output_to_operand_aliasing={{}: (2, {})} | custom-call | tf_op jit(solution)/shard_map/down/pallas_call | solution.py:421
  75.4 2.0 %collective-permute-done.12.refs_1_ = bf16[240,512]{1,0:T(8,128)(2,1)S(1)} collective-permute-done((bf16[240,512]{1,0:T(8,128)(2,1)S(1)}, bf16[240,512]{1,0:T(8,128)(2,1)S(1)}, u32[]{:S(2)}, u32[]{:S(2)}) %collective-permute-start.12) | collective-permute-done | bytes 245792 | tf_op jit(solution)/shard_map/ppermute | solution.py:311
  77.5 1.5 %down.5 = (bf16[60,1792]{1,0:T(8,128)(2,1)S(1)}, bf16[60,1792]{1,0:T(8,128)(2,1)S(1)}, bf16[60,1792]{1,0:T(8,128)(2,1)S(1)}, bf16[60,1792]{1,0:T(8,128)(2,1)S(1)}, f32[240,1792]{1,0:T(8,128)S(1)}) custom-call(s32[2]{0:T(128)S(1)} %pad_add_fusion.me_ref.place_ref, bf16[2048,1792]{1,0:T(8,128)(2,1)S(1)} %bitcast.11, ...), custom_call_target="tpu_custom_call", output_to_operand_aliasing={{4}: (2, {})} | custom-call | tf_op jit(solution)/shard_map/down/pallas_call | solution.py:421
  79.1 1.6 %collective-permute-start.14 = (bf16[60,1792]{1,0:T(8,128)(2,1)S(1)}, bf16[60,1792]{1,0:T(8,128)(2,1)S(1)}, u32[]{:S(2)}, u32[]{:S(2)}) collective-permute-start(bf16[60,1792]{1,0:T(8,128)(2,1)S(1)} %get-tuple-element.23), channel_id=1, source_target_pairs={{0,8},{4,12},{8,0},{12,4},{1,9},{5,13},{9,1},{13,5},{2,10},{6,14},... | collective-permute-start | bytes 645128 | tf_op jit(solution)/shard_map/ppermute | solution.py:308
  82.1 5.5 %collective-permute-done.14.refs_2_ = bf16[60,1792]{1,0:T(8,128)(2,1)S(1)} collective-permute-done((bf16[60,1792]{1,0:T(8,128)(2,1)S(1)}, bf16[60,1792]{1,0:T(8,128)(2,1)S(1)}, u32[]{:S(2)}, u32[]{:S(2)}) %collective-permute-start.14) | collective-permute-done | bytes 215072 | tf_op jit(solution)/shard_map/ppermute | solution.py:308
  87.6 3.8 %collective-permute-done.15.refs_3_ = bf16[60,1792]{1,0:T(8,128)(2,1)S(1)} collective-permute-done((bf16[60,1792]{1,0:T(8,128)(2,1)S(1)}, bf16[60,1792]{1,0:T(8,128)(2,1)S(1)}, u32[]{:S(2)}, u32[]{:S(2)}) %collective-permute-start.15) | collective-permute-done | bytes 215072 | tf_op jit(solution)/shard_map/ppermute | solution.py:308
  91.4 1.2 %combine.1 = bf16[96,1792]{1,0:T(8,128)(2,1)} custom-call(bf16[3,96,256]{2,1,0:T(8,128)(2,1)S(1)} %mixing.1.mixing_ref, bf16[60,1792]{1,0:T(8,128)(2,1)S(1)} %get-tuple-element.21.refs_0_, bf16[60,1792]{1,0:T(8,128)(2,1)S(1)} %collective-permute-done.13.refs_1_, bf16[60,1792]{1,0:T(8,128)(2,1)S(1)} %collective-permute-done.14.refs_2_, ...), custom_call_target="tpu_custom_call" | custom-call | tf_op jit(solution)/shard_map/combine/pallas_call | solution.py:440
  (38 shorter events, 7.0 us)
Async XLA Ops:
  2.0 13.2 %collective-permute-start = (bf16[60,1792]{1,0:T(8,128)(2,1)S(1)}, bf16[60,1792]{1,0:T(8,128)(2,1)S(1)}, u32[]{:S(2)}, u32[]{:S(2)}) collective-permute-start(bf16[60,1792]{1,0:T(8,128)(2,1)S(1)} %get-tuple-element.16), channel_id=1, source_target_pairs={{0,4},{4,0},{8,12},{12,8},{1,5},{5,1},{9,13},{13,9},{2,6},{6,2},{1... | collective-permute-start | bytes 645128 | tf_op jit(solution)/shard_map/ppermute | solution.py:308
  2.6 12.6 %collective-permute-start.1 = (bf16[60,1792]{1,0:T(8,128)(2,1)S(1)}, bf16[60,1792]{1,0:T(8,128)(2,1)S(1)}, u32[]{:S(2)}, u32[]{:S(2)}) collective-permute-start(bf16[60,1792]{1,0:T(8,128)(2,1)S(1)} %get-tuple-element.17), channel_id=1, source_target_pairs={{0,8},{4,12},{8,0},{12,4},{1,9},{5,13},{9,1},{13,5},{2,10},{6,14},... | collective-permute-start | bytes 645128 | tf_op jit(solution)/shard_map/ppermute | solution.py:308
  5.1 10.8 %collective-permute-start.2 = (bf16[60,1792]{1,0:T(8,128)(2,1)S(1)}, bf16[60,1792]{1,0:T(8,128)(2,1)S(1)}, u32[]{:S(2)}, u32[]{:S(2)}) collective-permute-start(bf16[60,1792]{1,0:T(8,128)(2,1)S(1)} %get-tuple-element.18), channel_id=1, source_target_pairs={{0,12},{4,8},{8,4},{12,0},{1,13},{5,9},{9,5},{13,1},{2,14},{6,10},... | collective-permute-start | bytes 645128 | tf_op jit(solution)/shard_map/ppermute | solution.py:308
  17.1 1.6 %copy-start = (bf16[240,1024]{1,0:T(8,128)(2,1)}, bf16[240,1024]{1,0:T(8,128)(2,1)S(1)}, u32[]{:S(2)}) copy-start(bf16[240,1024]{1,0:T(8,128)(2,1)S(1)} %first.1.refs_0_.first_ref) | copy-start | bytes 1474564
  17.1 13.4 %collective-permute-start.3 = (bf16[240,1024]{1,0:T(8,128)(2,1)S(1)}, bf16[240,1024]{1,0:T(8,128)(2,1)S(1)}, u32[]{:S(2)}, u32[]{:S(2)}) collective-permute-start(bf16[240,1024]{1,0:T(8,128)(2,1)S(1)} %first.1.refs_0_.first_ref), channel_id=1, source_target_pairs={{0,1},{1,0},{2,3},{3,2},{4,5},{5,4},{6,7},{7,6},{8,9},{9,8},{10,11... | collective-permute-start | bytes 1474568 | tf_op jit(solution)/shard_map/ppermute | solution.py:311
  18.7 53.6 %slice-start = ((s8[7340032]{0:T(1024)(128)(4,1)}), s8[4194304]{0:T(1024)(128)(4,1)S(1)}, s32[]{:S(2)}) async-start(s8[7340032]{0:T(1024)(128)(4,1)} %bitcast.7), calls=%async_computation | async-start | bytes 8388608
  23.7 1.0 %copy-start.1 = (bf16[240,1024]{1,0:T(8,128)(2,1)S(1)}, bf16[240,1024]{1,0:T(8,128)(2,1)}, u32[]{:S(2)}) copy-start(bf16[240,1024]{1,0:T(8,128)(2,1)} %copy-done) | copy-start | bytes 1474564
  24.7 47.5 %slice-start.1 = ((s8[7340032]{0:T(1024)(128)(4,1)}), s8[3145728]{0:T(1024)(128)(4,1)S(1)}, s32[]{:S(2)}) async-start(s8[7340032]{0:T(1024)(128)(4,1)} %bitcast.7), calls=%async_computation.1 | async-start | bytes 6291456
  28.2 13.3 %collective-permute-start.6 = (bf16[240,1024]{1,0:T(8,128)(2,1)S(1)}, bf16[240,1024]{1,0:T(8,128)(2,1)S(1)}, u32[]{:S(2)}, u32[]{:S(2)}) collective-permute-start(bf16[240,1024]{1,0:T(8,128)(2,1)S(1)} %get-tuple-element.20), channel_id=1, source_target_pairs={{0,1},{1,0},{2,3},{3,2},{4,5},{5,4},{6,7},{7,6},{8,9},{9,8},{10,11... | collective-permute-start | bytes 1474568 | tf_op jit(solution)/shard_map/ppermute | solution.py:311
  31.1 11.1 %collective-permute-start.4 = (bf16[240,1024]{1,0:T(8,128)(2,1)S(1)}, bf16[240,1024]{1,0:T(8,128)(2,1)S(1)}, u32[]{:S(2)}, u32[]{:S(2)}) collective-permute-start(bf16[240,1024]{1,0:T(8,128)(2,1)S(1)} %add.5), channel_id=1, source_target_pairs={{0,4},{1,2},{2,1},{3,7},{4,0},{5,6},{6,5},{7,3},{8,12},{9,10},{10,... | collective-permute-start | bytes 1474568 | tf_op jit(solution)/shard_map/ppermute | solution.py:311
  42.2 4.2 %collective-permute-start.7 = (bf16[240,1024]{1,0:T(8,128)(2,1)S(1)}, bf16[240,1024]{1,0:T(8,128)(2,1)S(1)}, u32[]{:S(2)}, u32[]{:S(2)}) collective-permute-start(bf16[240,1024]{1,0:T(8,128)(2,1)S(1)} %add.7), channel_id=1, source_target_pairs={{0,4},{1,2},{2,1},{3,7},{4,0},{5,6},{6,5},{7,3},{8,12},{9,10},{10,... | collective-permute-start | bytes 1474568 | tf_op jit(solution)/shard_map/ppermute | solution.py:311
  43.0 13.7 %collective-permute-start.5 = (bf16[240,1024]{1,0:T(8,128)(2,1)S(1)}, bf16[240,1024]{1,0:T(8,128)(2,1)S(1)}, u32[]{:S(2)}, u32[]{:S(2)}) collective-permute-start(bf16[240,1024]{1,0:T(8,128)(2,1)S(1)} %add.6), channel_id=1, source_target_pairs={{0,1},{1,0},{2,3},{3,2},{4,5},{5,4},{6,7},{7,6},{8,9},{9,8},{10,11... | collective-permute-start | bytes 1474568 | tf_op jit(solution)/shard_map/ppermute | solution.py:311
  57.6 6.3 %collective-permute-start.8 = (bf16[240,512]{1,0:T(8,128)(2,1)S(1)}, bf16[240,512]{1,0:T(8,128)(2,1)S(1)}, u32[]{:S(2)}, u32[]{:S(2)}) collective-permute-start(bf16[240,512]{1,0:T(8,128)(2,1)S(1)} %hidden.1.refs_0_), channel_id=1, source_target_pairs={{0,1},{1,0},{2,3},{3,2},{4,5},{5,4},{6,7},{7,6},{8,9},{9,8},{10,11... | collective-permute-start | bytes 737288 | tf_op jit(solution)/shard_map/ppermute | solution.py:311
  59.2 4.6 %collective-permute-start.9 = (bf16[240,512]{1,0:T(8,128)(2,1)S(1)}, bf16[240,512]{1,0:T(8,128)(2,1)S(1)}, u32[]{:S(2)}, u32[]{:S(2)}) collective-permute-start(bf16[240,512]{1,0:T(8,128)(2,1)S(1)} %hidden.1.refs_0_), channel_id=1, source_target_pairs={{0,4},{1,2},{2,1},{3,7},{4,0},{5,6},{6,5},{7,3},{8,12},{9,10},{10,... | collective-permute-start | bytes 737288 | tf_op jit(solution)/shard_map/ppermute | solution.py:311
  63.8 4.1 %collective-permute-start.11 = (bf16[240,512]{1,0:T(8,128)(2,1)S(1)}, bf16[240,512]{1,0:T(8,128)(2,1)S(1)}, u32[]{:S(2)}, u32[]{:S(2)}) collective-permute-start(bf16[240,512]{1,0:T(8,128)(2,1)S(1)} %collective-permute-done.8.refs_1_), channel_id=1, source_target_pairs={{0,4},{1,2},{2,1},{3,7},{4,0},{5,6},{6,5},{7,3},{8,12},{9,10},{10,... | collective-permute-start | bytes 737288 | tf_op jit(solution)/shard_map/ppermute | solution.py:311
  63.8 10.2 %collective-permute-start.10 = (bf16[240,512]{1,0:T(8,128)(2,1)S(1)}, bf16[240,512]{1,0:T(8,128)(2,1)S(1)}, u32[]{:S(2)}, u32[]{:S(2)}) collective-permute-start(bf16[240,512]{1,0:T(8,128)(2,1)S(1)} %collective-permute-done.9.refs_2_), channel_id=1, source_target_pairs={{0,1},{1,0},{2,3},{3,2},{4,5},{5,4},{6,7},{7,6},{8,9},{9,8},{10,11... | collective-permute-start | bytes 737288 | tf_op jit(solution)/shard_map/ppermute | solution.py:311
  68.0 9.5 %collective-permute-start.12 = (bf16[240,512]{1,0:T(8,128)(2,1)S(1)}, bf16[240,512]{1,0:T(8,128)(2,1)S(1)}, u32[]{:S(2)}, u32[]{:S(2)}) collective-permute-start(bf16[240,512]{1,0:T(8,128)(2,1)S(1)} %collective-permute-done.11.refs_2_), channel_id=1, source_target_pairs={{0,1},{1,0},{2,3},{3,2},{4,5},{5,4},{6,7},{7,6},{8,9},{9,8},{10,11... | collective-permute-start | bytes 737288 | tf_op jit(solution)/shard_map/ppermute | solution.py:311
  75.4 5.5 %copy-start.2 = (s32[96,2]{0,1:T(2,128)S(1)}, s32[96,2]{0,1:T(2,128)}, u32[]{:S(2)}) copy-start(s32[96,2]{0,1:T(2,128)} %param.6) | copy-start | bytes 2308
  75.4 5.6 %copy-start.3 = (f32[96,2]{0,1:T(2,128)S(1)}, f32[96,2]{0,1:T(2,128)}, u32[]{:S(2)}) copy-start(f32[96,2]{0,1:T(2,128)} %param.7) | copy-start | bytes 2308
  79.0 3.1 %collective-permute-start.13 = (bf16[60,1792]{1,0:T(8,128)(2,1)S(1)}, bf16[60,1792]{1,0:T(8,128)(2,1)S(1)}, u32[]{:S(2)}, u32[]{:S(2)}) collective-permute-start(bf16[60,1792]{1,0:T(8,128)(2,1)S(1)} %get-tuple-element.22), channel_id=1, source_target_pairs={{0,4},{4,0},{8,12},{12,8},{1,5},{5,1},{9,13},{13,9},{2,6},{6,2},{1... | collective-permute-start | bytes 645128 | tf_op jit(solution)/shard_map/ppermute | solution.py:308
  79.1 8.5 %collective-permute-start.14 = (bf16[60,1792]{1,0:T(8,128)(2,1)S(1)}, bf16[60,1792]{1,0:T(8,128)(2,1)S(1)}, u32[]{:S(2)}, u32[]{:S(2)}) collective-permute-start(bf16[60,1792]{1,0:T(8,128)(2,1)S(1)} %get-tuple-element.23), channel_id=1, source_target_pairs={{0,8},{4,12},{8,0},{12,4},{1,9},{5,13},{9,1},{13,5},{2,10},{6,14},... | collective-permute-start | bytes 645128 | tf_op jit(solution)/shard_map/ppermute | solution.py:308
  80.6 10.8 %collective-permute-start.15 = (bf16[60,1792]{1,0:T(8,128)(2,1)S(1)}, bf16[60,1792]{1,0:T(8,128)(2,1)S(1)}, u32[]{:S(2)}, u32[]{:S(2)}) collective-permute-start(bf16[60,1792]{1,0:T(8,128)(2,1)S(1)} %get-tuple-element.24), channel_id=1, source_target_pairs={{0,12},{4,8},{8,4},{12,0},{1,13},{5,9},{9,5},{13,1},{2,14},{6,10},... | collective-permute-start | bytes 645128 | tf_op jit(solution)/shard_map/ppermute | solution.py:308
